TPU v7x, 128 devices: a whole 4x4x4 slice. The times are simulated.
128 devices in a mesh: wide: 16 (over x_hi, z, core), narrow: 8 (over y, x_lo).
Axes of the slice: x: 4 (x_hi: 2, x_lo: 2; x = x_hi * 2 + x_lo), y: 4, z: 4, core: 2. Of those that a mesh axis runs over, the one named last changes fastest.
Arguments:
- replica_grads: bfloat16 [128, 16, 512, 512], P(('wide', 'narrow')), may hold values from -0.0625 to 0.0625
- owner_table: int32 [16], replicated, may hold values from 0 to 15, as said below
- left_stat: float32 [16, 512, 512], P('wide'), may hold values from -1 to 5, as said below
- right_stat: float32 [16, 512, 512], P('wide'), may hold values from -1 to 5, as said below
- left_root: float32 [16, 512, 512], P('wide'), may hold values from -1 to 2, as said below
- right_root: float32 [16, 512, 512], P('wide'), may hold values from -1 to 2, as said below
Outputs:
- directions: float32 [16, 512, 512], P(None, 'narrow')
- left_new: float32 [16, 512, 512], P('wide')
- right_new: float32 [16, 512, 512], P('wide')
- left_inverse: float32 [16, 512, 512], P('wide')
- right_inverse: float32 [16, 512, 512], P('wide')
Inputs may be any that keep to these rules, and one draw needn't show every extreme that they name: `owner_table`: the 16 entries are distinct, so every slot is named once. `left_stat`: each slot's matrix is symmetric positive definite. `right_stat`: each slot's matrix is symmetric positive definite. `left_root`: each slot's matrix is symmetric. `right_root`: each slot's matrix is symmetric.
All inputs are finite; a program needn't handle non-finite values.
Results may differ from a plain program's by a relative error of at most 0.0003.
Values sent between devices are 32-bit elements; how exact they have to be, the bound alone decides.
No kernel may reach another device: no remote copies, remote signals or barrier semaphores. Data moves between devices by JAX's collectives and lax.ppermute only.
A program may use at most 128 MiB of HBM per device.

v0:
```python
import jax
import jax.numpy as jnp
from jax import lax
from jax.sharding import PartitionSpec as P

decay_rate = 0.95


def matmul_high(first, second):
    return jnp.dot(
        first, second, precision=lax.Precision.HIGHEST, preferred_element_type=jnp.float32
    )


def gram_right(matrix):
    return lax.dot_general(
        matrix,
        matrix,
        (((0,), (0,)), ((), ())),
        precision=lax.Precision.HIGHEST,
        preferred_element_type=jnp.float32,
    )


def finish_newton(old_root, fourth_power, statistic):
    coupled = matmul_high(fourth_power, statistic)
    return (5.0 * old_root - matmul_high(old_root, coupled)) / 4.0


def local(replica_grads, owner_table, left_stat, right_stat, left_root, right_root):
    owners = lax.axis_size("wide")
    local_grads = replica_grads[0]
    order = local_grads.shape[1]
    selector = (owner_table[None, :] == jnp.arange(owners)[:, None]).astype(jnp.bfloat16)
    slot_grads = jnp.einsum(
        "wb,bij->wij", selector, local_grads, preferred_element_type=jnp.float32
    )
    left_prev = left_root[0]
    right_prev = right_root[0]
    left_squared = matmul_high(left_prev, left_prev)
    left_fourth = matmul_high(left_squared, left_squared)
    right_squared = matmul_high(right_prev, right_prev)
    right_fourth = matmul_high(right_squared, right_squared)
    partial_sum = lax.psum_scatter(slot_grads, "wide", scatter_dimension=0, tiled=True)[0]
    summed = lax.psum(partial_sum, "narrow")
    left_value = decay_rate * left_stat[0] + (1.0 - decay_rate) * matmul_high(summed, summed.T)
    right_value = decay_rate * right_stat[0] + (1.0 - decay_rate) * gram_right(summed)
    left_next = finish_newton(left_prev, left_fourth, left_value)
    right_next = finish_newton(right_prev, right_fourth, right_value)
    preconditioned = matmul_high(matmul_high(left_next, summed), right_next)
    piece_rows = order // lax.axis_size("narrow")
    row_start = lax.axis_index("narrow") * piece_rows
    own_rows = lax.dynamic_slice_in_dim(preconditioned, row_start, piece_rows, 0)
    gathered = lax.all_gather(own_rows[None], "wide", axis=0, tiled=True)
    directions = jnp.take(gathered, owner_table, axis=0)
    return (directions, left_value[None], right_value[None], left_next[None], right_next[None])


def solution(mesh):
    placed = (
        P(("wide", "narrow"), None, None, None),
        P(),
        P("wide", None, None),
        P("wide", None, None),
        P("wide", None, None),
        P("wide", None, None),
    )
    return jax.shard_map(
        local,
        mesh=mesh,
        in_specs=placed,
        out_specs=(
            P(None, "narrow", None),
            P("wide", None, None),
            P("wide", None, None),
            P("wide", None, None),
            P("wide", None, None),
        ),
        check_vma=False,
    )
```

profile of v0, /device:TPU:1, one launch (start us, length us, event | category | flops | bytes accessed | tf_op | source)
XLA Modules:
  0.0 346.2 jit_solution(1236870905349722525)
XLA Ops:
  7.2 0.0 reduce-scatter.2.cloned.1.call-start
  7.2 8.4 %fusion = f32[16,512,512]{2,0,1:T(8,128)S(1)} fusion(bf16[16,512,512]{2,1,0:T(8,128)(2,1)} %bitcast.68, s32[16]{0:T(128)} %param.7), kind=kOutput, calls=%fused_computation.1 | convolution fusion | flops 134217984 | bytes 25165888 | tf_op jit(solution)/shard_map/wb,bij->wij/dot_general | solution.py:35
  15.6 19.1 %copy.23 = f32[16,512,512]{2,1,0:T(8,128)} copy(f32[16,512,512]{2,0,1:T(8,128)S(1)} %fusion) | data formatting | bytes 33554432 | tf_op jit(solution)/shard_map/wb,bij->wij/dot_general | solution.py:35
  34.7 0.0 reduce-scatter.2.cloned.1.call-update
  34.8 0.0 all-reduce.2.cloned.1.call-start
  34.8 1.1 copy-done.1
  36.0 1.3 copy.21
  37.3 1.3 copy.24
  38.6 146.1 %reduce-scatter.2.cloned.1.call-done = f32[1,512,512]{2,1,0:T(8,128)} async-done(((f32[16,512,512]{2,1,0:T(8,128)}), f32[1,512,512]{2,1,0:T(8,128)}) %reduce-scatter.2.cloned.1.call-update) | async-done | bytes 1048592 | tf_op jit(solution)/shard_map/reduce_scatter | solution.py:44
  184.7 0.0 all-reduce.2.cloned.1.call-update
  184.7 0.2 all-gather.3.cloned.1.call-start
  184.9 1.8 fusion.12
  186.8 1.8 fusion.9
  188.6 1.8 fusion.17
  190.5 2.8 fusion.20
  193.3 68.5 %all-reduce.2.cloned.1.call-done = f32[512,512]{1,0:T(8,128)} async-done(((f32[512,512]{1,0:T(8,128)}), f32[512,512]{1,0:T(8,128)}) %all-reduce.2.cloned.1.call-update) | async-done | bytes 1048592 | tf_op jit(solution)/shard_map/psum | solution.py:45
  261.8 3.7 %fusion.7 = f32[512,512]{1,0:T(8,128)S(1)} fusion(f32[512,512]{1,0:T(8,128)} %all-reduce.2.cloned.1.call-done, f32[1,512,512]{2,1,0:T(8,128)} %param.8), kind=kOutput, calls=%fused_computation.12 | convolution fusion | flops 1611399168 | bytes 3145728 | tf_op jit(solution)/shard_map/dot_general | solution.py:10
  265.5 1.0 copy-done.4
  266.5 1.8 fusion.18
  268.4 3.7 %fusion.6 = f32[512,512]{0,1:T(8,128)S(1)} fusion(f32[512,512]{1,0:T(8,128)S(1)} %fusion.18, f32[1,512,512]{2,1,0:T(8,128)S(1)} %copy-done.1, f32[1,512,512]{1,2,0:T(8,128)S(1)} %copy-done.7), kind=kOutput, calls=%fused_computation.10 | convolution fusion | flops 1611399168 | bytes 4194304 | tf_op jit(solution)/shard_map/dot_general | solution.py:10
  272.1 1.9 fusion.4
  274.0 1.8 fusion.21
  275.9 3.5 %fusion.3 = f32[512,512]{0,1:T(8,128)S(1)} fusion(f32[512,512]{1,0:T(8,128)S(1)} %fusion.21, f32[1,512,512]{2,1,0:T(8,128)S(1)} %copy-done.2, f32[1,512,512]{1,2,0:T(8,128)S(1)} %copy-done.6), kind=kOutput, calls=%fused_computation.5 | convolution fusion | flops 1611399168 | bytes 4194304 | tf_op jit(solution)/shard_map/dot_general | solution.py:10
  279.4 1.8 fusion.19
  281.3 1.9 fusion.22
  283.2 0.7 constant_dynamic-slice_fusion
  283.8 0.0 all-gather.3.cloned.1.call-update
  283.9 1.3 copy.25
  285.2 1.3 copy.26
  286.5 49.1 %all-gather.3.cloned.1.call-done = f32[1024,512]{1,0:T(8,128)} async-done(((f32[64,512]{1,0:T(8,128)}), f32[1024,512]{1,0:T(8,128)}) %all-gather.3.cloned.1.call-update) | async-done | bytes 2097168 | tf_op jit(solution)/shard_map/all_gather | solution.py:54
  335.6 2.3 gather_fusion
  337.9 1.7 broadcast_select_fusion
  (21 shorter events, 0.1 us)
Async XLA Ops:
  7.2 177.5 %reduce-scatter.2.cloned.1.call-start = ((), (), s32[]{:S(2)}) async-start(), calls=%async_computation.1 | async-start | bytes 17825792 | tf_op jit(solution)/shard_map/reduce_scatter | solution.py:44
  34.7 1.2 copy-start.1
  34.8 2.5 copy-start.2
  34.8 227.0 %all-reduce.2.cloned.1.call-start = ((), (), s32[]{:S(2)}) async-start(), calls=%async_computation.2 | async-start | bytes 2097152 | tf_op jit(solution)/shard_map/psum | solution.py:45
  184.7 150.9 %all-gather.3.cloned.1.call-start = ((), (), s32[]{:S(2)}) async-start(), calls=%async_computation.3 | async-start | bytes 2228224 | tf_op jit(solution)/shard_map/all_gather | solution.py:54
  265.5 1.0 copy-start.4
  266.5 1.9 copy-start.7
  268.3 3.7 %copy-start = (f32[512,512]{1,0:T(8,128)S(1)}, f32[512,512]{1,0:T(8,128)}, u32[]{:S(2)}) copy-start(f32[512,512]{1,0:T(8,128)} %all-reduce.2.cloned.1.call-done) | copy-start | bytes 3145732
  268.4 3.7 %copy-start.8 = (f32[1,512,512]{2,1,0:T(8,128)S(1)}, f32[1,512,512]{2,1,0:T(8,128)}, u32[]{:S(2)}) copy-start(f32[1,512,512]{2,1,0:T(8,128)} %param.9) | copy-start | bytes 3145732
  272.1 1.9 copy-start.3
  274.0 5.4 %copy-start.5 = (f32[512,512]{1,0:T(8,128)}, f32[512,512]{1,0:T(8,128)S(1)}, u32[]{:S(2)}) copy-start(f32[512,512]{1,0:T(8,128)S(1)} %fusion.4) | copy-start | bytes 3145732
  274.0 1.9 copy-start.6
  281.3 2.6 copy-start.9
Sparse Core Ops, SparseCore 0:
  34.9 149.7 reduce-scatter.1
  187.2 74.5 all-reduce.1
  284.0 51.5 all-gather.2
where the time goes:
time: 346 us
  waiting for transfers between devices  264 us (76%)
  matrix products  37 us (11%)
  local copies, waits for them, and re-layouts  29.4 us (8%)
  between operations  14 us (4%)
    reduce_scatter x1, waiting for transfers between devices, local(): lax.psum_scatter(slot_grads, 'wide', scatter_dimension=0, tiled=True)[0]  146 us
    psum x1, waiting for transfers between devices, local(): summed = lax.psum(partial_sum, 'narrow')  68.5 us
    all_gather x1, waiting for transfers between devices, local(): gathered = lax.all_gather(own_rows[None], 'wide', axis=0, tiled=True)  49.1 us
    dot_general x11, matrix products, matmul_high(): jnp.dot(first, second, precision=lax.Precision.HIGHEST, preferred_element...  26.7 us
    dot_general x1, local copies, waits for them, and re-layouts, local(): jnp.einsum('wb,bij->wij', selector, local_grads, preferred_element_type=j...  19.1 us
    dot_general x1, matrix products, local(): jnp.einsum('wb,bij->wij', selector, local_grads, preferred_element_type=j...  8.42 us
    unnamed x24, local copies, waits for them, and re-layouts  7.37 us
  transfers between devices with their start and end apart: 3, of which 3 were waited for; matrix products, arithmetic and copies ran while one was open for 4% of the time, Pallas kernels for 0%

commit v1 on v0

--- a/solution.py
+++ b/solution.py
@@ -42,7 +42,7 @@
     right_squared = matmul_high(right_prev, right_prev)
     right_fourth = matmul_high(right_squared, right_squared)
     partial_sum = lax.psum_scatter(slot_grads, "wide", scatter_dimension=0, tiled=True)[0]
-    summed = lax.psum(partial_sum, "narrow")
+    summed = jnp.sum(lax.all_gather(partial_sum, "narrow"), axis=0)
     left_value = decay_rate * left_stat[0] + (1.0 - decay_rate) * matmul_high(summed, summed.T)
     right_value = decay_rate * right_stat[0] + (1.0 - decay_rate) * gram_right(summed)
     left_next = finish_newton(left_prev, left_fourth, left_value)

time: 346 us -> 446 us (1.29); the launches traced: 346 us -> 438 us
  waiting for transfers between devices: 264 us -> 353 us
  other arithmetic: 1.76 us -> 6.25 us
    all_gather x0 -> x1, waiting for transfers between devices: none -> 157 us  [local(): summed = jnp.sum(lax.all_gather(partial_sum, 'narrow'), axis=0)]
    psum x1 -> x0, waiting for transfers between devices: 68.5 us -> none  [local(): summed = lax.psum(partial_sum, 'narrow')]
    reduce_sum x0 -> x1, other arithmetic: none -> 4.49 us  [local(): summed = jnp.sum(lax.all_gather(partial_sum, 'narrow'), axis=0)]
  transfers between devices with their start and end apart: 3 -> 3, of which waited for: 3 -> 3; matrix products, arithmetic and copies ran while one was open for 4% -> 3% of each run, Pallas kernels for 0% -> 0%
where the time goes in v1:
time: 446 us; the launch traced here: 438 us
  waiting for transfers between devices  353 us (79%)
  matrix products  36.5 us (8%)
  local copies, waits for them, and re-layouts  27.4 us (6%)
  between operations  14.2 us (3%)
  other arithmetic  6.25 us (1%)
    all_gather x1, waiting for transfers between devices, local(): summed = jnp.sum(lax.all_gather(partial_sum, 'narrow'), axis=0)  157 us
    reduce_scatter x1, waiting for transfers between devices, local(): lax.psum_scatter(slot_grads, 'wide', scatter_dimension=0, tiled=True)[0]  150 us
    all_gather x1, waiting for transfers between devices, local(): gathered = lax.all_gather(own_rows[None], 'wide', axis=0, tiled=True)  46.5 us
    dot_general x11, matrix products, matmul_high(): jnp.dot(first, second, precision=lax.Precision.HIGHEST, preferred_element...  26.2 us
    dot_general x1, local copies, waits for them, and re-layouts, local(): jnp.einsum('wb,bij->wij', selector, local_grads, preferred_element_type=j...  19.1 us
  transfers between devices with their start and end apart: 3, of which 3 were waited for; matrix products, arithmetic and copies ran while one was open for 3% of the time, Pallas kernels for 0%

profile of v1, /device:TPU:1, one launch (start us, length us, event | category | flops | bytes accessed | tf_op | source)
XLA Modules:
  0.0 438.3 jit_solution(10063932992495899374)
XLA Ops:
  7.2 0.0 reduce-scatter.2.cloned.1.call-start
  7.2 8.4 %fusion = f32[16,512,512]{2,0,1:T(8,128)S(1)} fusion(bf16[16,512,512]{2,1,0:T(8,128)(2,1)} %bitcast.67, s32[16]{0:T(128)} %param.7), kind=kOutput, calls=%fused_computation.1 | convolution fusion | flops 134217984 | bytes 25165888 | tf_op jit(solution)/shard_map/wb,bij->wij/dot_general | solution.py:35
  15.6 19.1 %copy.23 = f32[16,512,512]{2,1,0:T(8,128)} copy(f32[16,512,512]{2,0,1:T(8,128)S(1)} %fusion) | data formatting | bytes 33554432 | tf_op jit(solution)/shard_map/wb,bij->wij/dot_general | solution.py:35
  34.7 0.0 reduce-scatter.2.cloned.1.call-update
  34.8 0.0 all-gather.4.cloned.1.call-start
  34.8 150.0 %reduce-scatter.2.cloned.1.call-done = f32[1,512,512]{2,1,0:T(8,128)} async-done(((f32[16,512,512]{2,1,0:T(8,128)}), f32[1,512,512]{2,1,0:T(8,128)}) %reduce-scatter.2.cloned.1.call-update) | async-done | bytes 1048592 | tf_op jit(solution)/shard_map/reduce_scatter | solution.py:44
  184.8 0.0 all-gather.4.cloned.1.call-update
  184.8 0.5 all-gather.6.cloned.1.call-start
  185.3 1.3 copy.21
  186.6 1.3 copy.24
  187.9 1.8 fusion.12
  189.8 1.8 fusion.9
  191.6 1.8 fusion.17
  193.5 2.8 fusion.20
  196.3 156.8 %all-gather.4.cloned.1.call-done = f32[8,512,512]{2,1,0:T(8,128)} async-done(((f32[1,512,512]{2,1,0:T(8,128)}), f32[8,512,512]{2,1,0:T(8,128)}) %all-gather.4.cloned.1.call-update) | async-done | bytes 8388624 | tf_op jit(solution)/shard_map/all_gather | solution.py:45
  353.1 4.5 %reduce_sum.9 = f32[512,512]{1,0:T(8,128)S(1)} reduce(f32[8,512,512]{2,1,0:T(8,128)} %all-gather.4.cloned.1.call-done, f32[]{:T(128)} %constant.10.clone.1), dimensions={0}, to_apply=%region_1.0 | reduce | flops 1835008 | bytes 9437188 | tf_op jit(solution)/shard_map/reduce_sum | solution.py:45
  357.6 3.1 fusion.7
  360.8 1.8 fusion.18
  362.6 3.6 fusion.6
  366.3 1.8 fusion.19
  368.2 1.9 fusion.4
  370.2 1.8 fusion.21
  372.0 0.0 copy-done.6
  372.1 3.5 fusion.3
  375.6 2.1 fusion.22
  377.7 0.7 constant_dynamic-slice_fusion
  378.3 0.0 all-gather.6.cloned.1.call-update
  378.4 1.3 copy.25
  379.7 1.3 copy.26
  381.0 46.5 %all-gather.6.cloned.1.call-done = f32[1024,512]{1,0:T(8,128)} async-done(((f32[64,512]{1,0:T(8,128)}), f32[1024,512]{1,0:T(8,128)}) %all-gather.6.cloned.1.call-update) | async-done | bytes 2097168 | tf_op jit(solution)/shard_map/all_gather | solution.py:54
  427.6 2.3 gather_fusion
  429.8 1.7 broadcast_select_fusion
  (22 shorter events, 0.1 us)
Async XLA Ops:
  7.2 177.6 %reduce-scatter.2.cloned.1.call-start = ((), (), s32[]{:S(2)}) async-start(), calls=%async_computation.1 | async-start | bytes 17825792 | tf_op jit(solution)/shard_map/reduce_scatter | solution.py:44
  34.7 150.6 %copy-start = (f32[1,512,512]{2,1,0:T(8,128)S(1)}, f32[1,512,512]{2,1,0:T(8,128)}, u32[]{:S(2)}) copy-start(f32[1,512,512]{2,1,0:T(8,128)} %param.10) | copy-start | bytes 3145732
  34.8 151.9 %copy-start.1 = (f32[1,512,512]{2,1,0:T(8,128)S(1)}, f32[1,512,512]{2,1,0:T(8,128)}, u32[]{:S(2)}) copy-start(f32[1,512,512]{2,1,0:T(8,128)} %param.11) | copy-start | bytes 3145732
  34.8 318.4 %all-gather.4.cloned.1.call-start = ((), (), s32[]{:S(2)}) async-start(), calls=%async_computation.2 | async-start | bytes 9437184 | tf_op jit(solution)/shard_map/all_gather | solution.py:45
  184.8 242.8 %all-gather.6.cloned.1.call-start = ((), (), s32[]{:S(2)}) async-start(), calls=%async_computation.3 | async-start | bytes 2228224 | tf_op jit(solution)/shard_map/all_gather | solution.py:54
  360.8 5.6 %copy-start.4 = (f32[512,512]{1,0:T(8,128)}, f32[512,512]{1,0:T(8,128)S(1)}, u32[]{:S(2)}) copy-start(f32[512,512]{1,0:T(8,128)S(1)} %fusion.7) | copy-start | bytes 3145732
  360.8 1.9 copy-start.7
  366.3 1.9 copy-start.8
  368.2 1.9 copy-start.3
  370.1 5.4 %copy-start.5 = (f32[512,512]{1,0:T(8,128)}, f32[512,512]{1,0:T(8,128)S(1)}, u32[]{:S(2)}) copy-start(f32[512,512]{1,0:T(8,128)S(1)} %fusion.4) | copy-start | bytes 3145732
  370.1 1.9 copy-start.2
  370.1 1.9 copy-start.6
  375.6 2.8 copy-start.9
Sparse Core Ops, SparseCore 0:
  34.9 149.8 reduce-scatter.1
  186.4 166.6 all-gather.3
  378.5 49.0 all-gather.5
